TPU v7x, 512 devices: a whole 4x8x8 slice. The times are simulated.
512 devices in a mesh: scen: 8 (over x, core), bus: 64 (over y, z).
Axes of the slice: x: 4, y: 8, z: 8, core: 2. Of those that a mesh axis runs over, the one named last changes fastest.
Arguments:
- injections: bfloat16 [1024, 16384], P(('scen', 'bus')), may hold values from -6 to 6
- tile_values: bfloat16 [4096, 128, 128], P('bus', 'scen'), may hold values from -0.109375 to 0.109375
- tile_line: int32 [4096], P('bus'), may hold values from 0 to 191, as said below
- tile_bus: int32 [4096], P('bus'), may hold values from 0 to 1
- flow_pred: bfloat16 [1024, 24576], P('scen', 'bus'), may hold values from -6 to 6
- line_limit: int32 [24576], P('bus'), may hold values from 50 to 199
Outputs:
- grad_injections: bfloat16 [1024, 16384], P(('scen', 'bus'))
- flows: float32 [1024, 24576], P('scen', 'bus')
Inputs may be any that keep to these rules, and one draw needn't show every extreme that they name: `tile_line`: tile t is held by bus index t // 64; line block b is owned by bus index b // 3. Of the 64 tiles of one bus index at most 2 have line blocks of one owner, and in every draw some owner gets exactly 2 tiles from every bus index. A pair of line block and bus block may occur in several tiles; their values add.
All inputs are finite; a program needn't handle non-finite values.
Results may differ from a plain program's by a relative error of at most 0.0039.
Values may be sent and summed in bfloat16 or wider, within the bound.
No kernel may reach another device: no remote copies, remote signals or barrier semaphores. Data moves between devices by JAX's collectives and lax.ppermute only.
A program may use at most 64 MiB of HBM per device.

v0:
```python
import jax
import jax.numpy as jnp
from jax import lax
from jax.sharding import PartitionSpec as P


def per_device(injections, tile_values, tile_line, tile_bus, flow_pred, line_limit):
    bus_count = lax.axis_size("bus")
    local_inj = lax.all_to_all(injections, "bus", split_axis=1, concat_axis=0, tiled=True)
    tile_full = lax.all_gather(tile_values, "scen", axis=1, tiled=True)
    tile_count = tile_full.shape[0]
    tile_size = tile_full.shape[1]
    row_count = local_inj.shape[0]
    blocks_here = local_inj.shape[1] // tile_size
    line_blocks = flow_pred.shape[1] // tile_size
    per_owner = tile_count // bus_count
    capacity = per_owner + max(1, tile_count // (2 * bus_count))
    slot_total = bus_count * capacity
    inj_blocks = local_inj.reshape(row_count, blocks_here, tile_size)
    per_tile_inj = jnp.take(inj_blocks, tile_bus, axis=1)
    partial_flows = jnp.einsum(
        "stb,tlb->tsl", per_tile_inj, tile_full, preferred_element_type=jnp.float32
    )
    owner_index = tile_line // line_blocks
    within_owner = tile_line % line_blocks
    owner_hits = (owner_index[:, None] == jnp.arange(bus_count, dtype=jnp.int32)[None, :]).astype(
        jnp.int32
    )
    rank_within = jnp.sum(jnp.cumsum(owner_hits, axis=0) * owner_hits, axis=1) - 1
    slot_index = owner_index * capacity + rank_within
    send_buffer = (
        jnp.zeros((slot_total, row_count, tile_size), jnp.float32).at[slot_index].set(partial_flows)
    )
    slot_label = jnp.full((slot_total,), -1, jnp.int32).at[slot_index].set(within_owner)
    received, received_label = (
        lax.all_to_all(send_buffer, "bus", split_axis=0, concat_axis=0, tiled=True),
        lax.all_to_all(slot_label, "bus", split_axis=0, concat_axis=0, tiled=True),
    )
    select_mask = (
        received_label[None, :] == jnp.arange(line_blocks, dtype=jnp.int32)[:, None]
    ).astype(jnp.float32)
    flow_blocks = jnp.einsum("ms,srl->rml", select_mask, received, precision=lax.Precision.HIGHEST)
    flows = flow_blocks.reshape(row_count, line_blocks * tile_size)
    line_cap = line_limit.astype(jnp.float32) * 0.01
    residual = flows - flow_pred.astype(jnp.float32)
    grad_flow = (
        residual
        + jax.nn.sigmoid(4.0 * (flows - line_cap))
        - jax.nn.sigmoid(4.0 * (-flows - line_cap))
    ).astype(jnp.bfloat16)
    gathered = lax.all_gather(grad_flow, "bus", axis=1, tiled=True)
    gathered_blocks = gathered.reshape(row_count, gathered.shape[1] // tile_size, tile_size)
    per_tile_grad = jnp.take(gathered_blocks, tile_line, axis=1)
    contrib = jnp.einsum(
        "stl,tlb->stb", per_tile_grad, tile_full, preferred_element_type=jnp.float32
    )
    bus_select = (tile_bus[:, None] == jnp.arange(blocks_here, dtype=jnp.int32)[None, :]).astype(
        jnp.float32
    )
    grad_blocks_bus = jnp.einsum(
        "stb,tk->skb", contrib, bus_select, precision=lax.Precision.HIGHEST
    )
    grad_local = grad_blocks_bus.reshape(row_count, blocks_here * tile_size).astype(jnp.bfloat16)
    grad_injections = lax.all_to_all(grad_local, "bus", split_axis=0, concat_axis=1, tiled=True)
    return (grad_injections, flows)


def solution(mesh):
    return jax.shard_map(
        per_device,
        mesh=mesh,
        in_specs=(
            P(("scen", "bus"), None),
            P("bus", "scen", None),
            P("bus"),
            P("bus"),
            P("scen", "bus"),
            P("bus"),
        ),
        out_specs=(P(("scen", "bus"), None), P("scen", "bus")),
        check_vma=False,
    )
```

profile of v0, /device:TPU:2, one launch (start us, length us, event | category | flops | bytes accessed | tf_op | source)
XLA Modules:
  0.0 535.0 jit_solution(14193557377811817124)
XLA Ops:
  7.2 0.0 all-gather.3.cloned.1.call-start
  7.2 0.7 all-gather.3.cloned.1.call-update
  7.9 16.6 %all-to-all-start = ((bf16[2,64,256]{2,0,1:T(2,128)(2,1)}), bf16[2,64,256]{2,0,1:T(2,128)(2,1)S(1)}, u32[]{:S(2)}, u32[]{:S(2)}) async-start(bf16[2,64,256]{2,0,1:T(2,128)(2,1)} %bitcast.34), calls=%async_computation | async-start | bytes 131072 | tf_op jit(solution)/shard_map/all_to_all | solution.py:9
  24.5 0.7 compare_select_fusion.2
  25.2 0.1 fusion.22
  25.3 0.1 reduce_window_sum.11
  25.3 0.2 select_reduce_fusion
  25.5 0.7 compare_select_fusion
  26.2 0.7 compare_and_fusion
  26.9 0.8 scatter_custom_fusion.1
  27.6 0.8 all_to_all.37
  28.4 8.4 %all-to-all-done = bf16[2,64,256]{2,0,1:T(2,128)(2,1)S(1)} async-done(((bf16[2,64,256]{2,0,1:T(2,128)(2,1)}), bf16[2,64,256]{2,0,1:T(2,128)(2,1)S(1)}, u32[]{:S(2)}, u32[]{:S(2)}) %all-to-all-start) | async-done | bytes 65568 | tf_op jit(solution)/shard_map/all_to_all | solution.py:9
  36.8 4.6 all-to-all-start.2
  41.4 1.0 gather_fusion
  42.4 4.4 all-gather.3.cloned.1.call-done
  46.9 5.2 fusion.5
  52.0 4.3 broadcast_in_dim.41
  56.3 12.0 %scatter_fusion = f32[128,128,128]{2,1,0:T(8,128)} fusion(f32[128,128,128]{2,1,0:T(8,128)} %broadcast_in_dim.41, s32[64]{0:T(128)S(1)} %compare_select_fusion.1, f32[64,128,128]{2,1,0:T(8,128)} %fusion.5), kind=kCustom, calls=%fused_computation.2 | custom fusion | bytes 12583168 | tf_op jit(solution)/shard_map/scatter | solution.py:32
  68.3 0.0 copy-start
  68.3 0.0 copy-start.1
  68.4 0.0 all-to-all-done.2
  68.4 13.8 %all-to-all-start.1 = ((f32[128,128,128]{2,1,0:T(8,128)}), f32[128,128,128]{2,1,0:T(8,128)}, u32[]{:S(2)}, u32[]{:S(2)}) async-start(f32[128,128,128]{2,1,0:T(8,128)} %scatter_fusion), calls=%async_computation.1 | async-start | bytes 16777216 | tf_op jit(solution)/shard_map/all_to_all | solution.py:36
  82.1 0.2 all-gather.5.cloned.1.call-start
  82.4 0.0 copy-done
  82.4 0.1 copy.30
  82.5 0.0 copy-done.1
  82.5 0.5 broadcast.71
  83.0 0.7 reduce.3
  83.8 0.1 eq.49
  83.9 0.0 copy-start.3
  83.9 234.9 %all-to-all-done.1 = f32[128,128,128]{2,1,0:T(8,128)} async-done(((f32[128,128,128]{2,1,0:T(8,128)}), f32[128,128,128]{2,1,0:T(8,128)}, u32[]{:S(2)}, u32[]{:S(2)}) %all-to-all-start.1) | async-done | bytes 8388640 | tf_op jit(solution)/shard_map/all_to_all | solution.py:36
  318.8 10.4 %fusion.11 = f32[128,3,128]{2,1,0:T(4,128)S(1)} fusion(f32[128,128,128]{2,1,0:T(8,128)} %all-to-all-done.1, s32[128]{0:T(128)S(1)} %eq.49), kind=kOutput, calls=%fused_computation.16 | convolution fusion | flops 75497856 | bytes 8585728 | tf_op jit(solution)/shard_map/ms,srl->rml/dot_general | solution.py:42
  329.2 0.1 copy.29
  329.4 0.8 subtract_convert_fusion
  330.2 0.0 all-gather.5.cloned.1.call-update
  330.2 0.0 copy-done.3
  330.3 157.1 %all-gather.5.cloned.1.call-done = bf16[128,24576]{0,1:T(8,128)(2,1)} async-done(((bf16[128,384]{0,1:T(8,128)(2,1)}), bf16[128,24576]{0,1:T(8,128)(2,1)}) %all-gather.5.cloned.1.call-update) | async-done | bytes 6291472 | tf_op jit(solution)/shard_map/all_gather | solution.py:51
  487.4 8.7 %copy.31 = bf16[128,192,128]{2,0,1:T(8,128)(2,1)} copy(bf16[128,192,128]{0,2,1:T(8,128)(2,1)} %bitcast.30) | data formatting | bytes 12582912 | tf_op jit(solution)/shard_map/reshape | solution.py:52
  496.0 3.7 gather_fusion.1
  499.8 0.0 copy-start.2
  499.8 2.4 convolution_bitcast_fusion
  502.1 0.0 copy-done.2
  502.1 3.8 fusion.17
  506.0 0.7 convert_element_type.30
  506.6 8.6 %all-to-all-start.3 = ((bf16[64,2,256]{2,1,0:T(2,128)(2,1)}), bf16[64,2,256]{2,1,0:T(2,128)(2,1)S(1)}, u32[]{:S(2)}, u32[]{:S(2)}) async-start(bf16[64,2,256]{2,1,0:T(2,128)(2,1)} %convert_element_type.30), calls=%async_computation.3 | async-start | bytes 131072 | tf_op jit(solution)/shard_map/all_to_all | solution.py:64
  515.2 0.8 copy.34
  516.0 11.5 %all-to-all-done.3 = bf16[64,2,256]{2,1,0:T(2,128)(2,1)S(1)} async-done(((bf16[64,2,256]{2,1,0:T(2,128)(2,1)}), bf16[64,2,256]{2,1,0:T(2,128)(2,1)S(1)}, u32[]{:S(2)}, u32[]{:S(2)}) %all-to-all-start.3) | async-done | bytes 65568 | tf_op jit(solution)/shard_map/all_to_all | solution.py:64
  527.5 0.6 copy.47
  (7 shorter events, 0.1 us)
Async XLA Ops:
  7.2 39.7 %all-gather.3.cloned.1.call-start = ((), (), s32[]{:S(2)}) async-start(), calls=%async_computation.4 | async-start | bytes 2359296 | tf_op jit(solution)/shard_map/all_gather | solution.py:10
  7.9 28.9 %all-to-all-start = ((bf16[2,64,256]{2,0,1:T(2,128)(2,1)}), bf16[2,64,256]{2,0,1:T(2,128)(2,1)S(1)}, u32[]{:S(2)}, u32[]{:S(2)}) async-start(bf16[2,64,256]{2,0,1:T(2,128)(2,1)} %bitcast.34), calls=%async_computation | async-start | bytes 131072 | tf_op jit(solution)/shard_map/all_to_all | solution.py:9
  36.8 31.6 %all-to-all-start.2 = ((s32[64,2,1]{1,2,0:T(1,128)}), s32[64,2,1]{1,2,0:T(1,128)S(1)}, u32[]{:S(2)}, u32[]{:S(2)}) async-start(s32[64,2,1]{1,2,0:T(1,128)} %bitcast.4), calls=%async_computation.2 | async-start | bytes 65536 | tf_op jit(solution)/shard_map/all_to_all | solution.py:37
  68.3 14.0 %copy-start = (bf16[128,384]{1,0:T(8,128)(2,1)S(1)}, bf16[128,384]{1,0:T(8,128)(2,1)}, u32[]{:S(2)}) copy-start(bf16[128,384]{1,0:T(8,128)(2,1)} %param.10) | copy-start | bytes 294916
  68.3 14.1 %copy-start.1 = (s32[384]{0:T(512)S(1)}, s32[384]{0:T(512)}, u32[]{:S(2)}) copy-start(s32[384]{0:T(512)} %param.11) | copy-start | bytes 4612
  68.4 250.5 %all-to-all-start.1 = ((f32[128,128,128]{2,1,0:T(8,128)}), f32[128,128,128]{2,1,0:T(8,128)}, u32[]{:S(2)}, u32[]{:S(2)}) async-start(f32[128,128,128]{2,1,0:T(8,128)} %scatter_fusion), calls=%async_computation.1 | async-start | bytes 16777216 | tf_op jit(solution)/shard_map/all_to_all | solution.py:36
  82.1 405.2 %all-gather.5.cloned.1.call-start = ((), (), s32[]{:S(2)}) async-start(), calls=%async_computation.5 | async-start | bytes 6389760 | tf_op jit(solution)/shard_map/all_gather | solution.py:51
  83.9 246.4 %copy-start.3 = (s32[64]{0:T(128)S(1)}, s32[64]{0:T(128)}, u32[]{:S(2)}) copy-start(s32[64]{0:T(128)} %param.8) | copy-start | bytes 772
  499.8 2.4 copy-start.2
  506.6 20.9 %all-to-all-start.3 = ((bf16[64,2,256]{2,1,0:T(2,128)(2,1)}), bf16[64,2,256]{2,1,0:T(2,128)(2,1)S(1)}, u32[]{:S(2)}, u32[]{:S(2)}) async-start(bf16[64,2,256]{2,1,0:T(2,128)(2,1)} %convert_element_type.30), calls=%async_computation.3 | async-start | bytes 131072 | tf_op jit(solution)/shard_map/all_to_all | solution.py:64
Sparse Core Ops, SparseCore 0:
  10.1 36.6 all-gather.2
  330.4 156.9 all-gather.4
where the time goes:
time: 536 us; the launch traced here: 535 us
  waiting for transfers between devices  417 us (78%)
  starting transfers between devices  43.8 us (8%)
  local copies, waits for them, and re-layouts  34.3 us (6%)
  matrix products  21.8 us (4%)
  between operations  14.2 us (3%)
    all_to_all x1, waiting for transfers between devices, per_device(): lax.all_to_all(send_buffer, 'bus', split_axis=0, concat_axis=0, tiled=True)  235 us
    all_gather x1, waiting for transfers between devices, per_device(): gathered = lax.all_gather(grad_flow, 'bus', axis=1, tiled=True)  157 us
    all_to_all x1, starting transfers between devices, per_device(): lax.all_to_all(injections, 'bus', split_axis=1, concat_axis=0, tiled=True)  16.6 us
    all_to_all x1, starting transfers between devices, per_device(): lax.all_to_all(send_buffer, 'bus', split_axis=0, concat_axis=0, tiled=True)  13.8 us
    scatter x1, local copies, waits for them, and re-layouts, per_device(): jnp.zeros((slot_total, row_count, tile_size), jnp.float32).at[slot_index]  12 us
    all_to_all x1, waiting for transfers between devices, per_device(): lax.all_to_all(grad_local, 'bus', split_axis=0, concat_axis=1, tiled=True)  11.5 us
  transfers between devices with their start and end apart: 6, of which 5 were waited for; matrix products, arithmetic and copies ran while one was open for 5% of the time, Pallas kernels for 0%

commit v1 on v0

--- a/solution.py
+++ b/solution.py
@@ -48,7 +48,9 @@
         + jax.nn.sigmoid(4.0 * (flows - line_cap))
         - jax.nn.sigmoid(4.0 * (-flows - line_cap))
     ).astype(jnp.bfloat16)
-    gathered = lax.all_gather(grad_flow, "bus", axis=1, tiled=True)
+    gathered = jnp.concatenate(
+        lax.all_to_all(jnp.stack([grad_flow] * lax.axis_size("bus")), "bus", 0, 0), axis=1
+    )
     gathered_blocks = gathered.reshape(row_count, gathered.shape[1] // tile_size, tile_size)
     per_tile_grad = jnp.take(gathered_blocks, tile_line, axis=1)
     contrib = jnp.einsum(

time: 536 us -> 658 us (1.23)
  the two profiles are of different devices: /device:TPU:2 before, /device:TPU:8 now
where the time goes in v1:
time: 658 us; the launch traced here: 657 us
  waiting for transfers between devices  462 us (70%)
  starting transfers between devices  117 us (18%)
  local copies, waits for them, and re-layouts  38.3 us (6%)
  matrix products  21.7 us (3%)
  between operations  14.2 us (2%)
    all_to_all x1, waiting for transfers between devices, per_device(): lax.all_to_all(send_buffer, 'bus', split_axis=0, concat_axis=0, tiled=True)  250 us
    all_to_all x1, waiting for transfers between devices, per_device(): lax.all_to_all(jnp.stack([grad_flow] * lax.axis_size('bus')), 'bus', 0, 0)  188 us
    all_to_all x1, starting transfers between devices, per_device(): lax.all_to_all(jnp.stack([grad_flow] * lax.axis_size('bus')), 'bus', 0, 0)  49.9 us
    all_to_all x1, starting transfers between devices, per_device(): lax.all_to_all(grad_local, 'bus', split_axis=0, concat_axis=1, tiled=True)  31.7 us
    all_to_all x1, starting transfers between devices, per_device(): lax.all_to_all(injections, 'bus', split_axis=1, concat_axis=0, tiled=True)  16.6 us
    all_to_all x1, starting transfers between devices, per_device(): lax.all_to_all(send_buffer, 'bus', split_axis=0, concat_axis=0, tiled=True)  13.8 us
  transfers between devices with their start and end apart: 6, of which 5 were waited for; matrix products, arithmetic and copies ran while one was open for 4% of the time, Pallas kernels for 0%

profile of v1, /device:TPU:8, one launch (start us, length us, event | category | flops | bytes accessed | tf_op | source)
XLA Modules:
  0.0 656.7 jit_solution(9815568015619625779)
XLA Ops:
  7.2 0.0 all-gather.2.cloned.1.call-start
  7.2 0.7 all-gather.2.cloned.1.call-update
  7.9 16.6 %all-to-all-start = ((bf16[2,64,256]{2,0,1:T(2,128)(2,1)}), bf16[2,64,256]{2,0,1:T(2,128)(2,1)S(1)}, u32[]{:S(2)}, u32[]{:S(2)}) async-start(bf16[2,64,256]{2,0,1:T(2,128)(2,1)} %bitcast.35), calls=%async_computation | async-start | bytes 131072 | tf_op jit(solution)/shard_map/all_to_all | solution.py:9
  24.5 0.7 compare_select_fusion.2
  25.2 0.1 fusion.22
  25.2 0.1 reduce_window_sum.11
  25.3 0.2 select_reduce_fusion
  25.5 0.7 compare_select_fusion
  26.2 0.7 compare_and_fusion
  26.9 0.8 scatter_custom_fusion.1
  27.6 0.8 all_to_all.40
  28.4 7.5 %all-to-all-done = bf16[2,64,256]{2,0,1:T(2,128)(2,1)S(1)} async-done(((bf16[2,64,256]{2,0,1:T(2,128)(2,1)}), bf16[2,64,256]{2,0,1:T(2,128)(2,1)S(1)}, u32[]{:S(2)}, u32[]{:S(2)}) %all-to-all-start) | async-done | bytes 65568 | tf_op jit(solution)/shard_map/all_to_all | solution.py:9
  35.9 5.4 all-to-all-start.2
  41.4 1.0 gather_fusion
  42.3 4.9 all-gather.2.cloned.1.call-done
  47.2 5.2 fusion.5
  52.4 4.3 broadcast_in_dim.41
  56.7 11.9 %scatter_fusion = f32[128,128,128]{2,1,0:T(8,128)} fusion(f32[128,128,128]{2,1,0:T(8,128)} %broadcast_in_dim.41, s32[64]{0:T(128)S(1)} %compare_select_fusion.1, f32[64,128,128]{2,1,0:T(8,128)} %fusion.5), kind=kCustom, calls=%fused_computation.2 | custom fusion | bytes 12583168 | tf_op jit(solution)/shard_map/scatter | solution.py:32
  68.6 0.0 copy-start
  68.6 0.0 copy-start.1
  68.6 0.0 all-to-all-done.2
  68.6 13.8 %all-to-all-start.1 = ((f32[128,128,128]{2,1,0:T(8,128)}), f32[128,128,128]{2,1,0:T(8,128)}, u32[]{:S(2)}, u32[]{:S(2)}) async-start(f32[128,128,128]{2,1,0:T(8,128)} %scatter_fusion), calls=%async_computation.1 | async-start | bytes 16777216 | tf_op jit(solution)/shard_map/all_to_all | solution.py:36
  82.5 0.0 copy-done
  82.5 0.1 copy.22
  82.6 0.0 copy-done.1
  82.6 0.5 broadcast.73
  83.1 0.7 reduce.3
  83.9 0.1 eq.49
  84.0 250.0 %all-to-all-done.1 = f32[128,128,128]{2,1,0:T(8,128)} async-done(((f32[128,128,128]{2,1,0:T(8,128)}), f32[128,128,128]{2,1,0:T(8,128)}, u32[]{:S(2)}, u32[]{:S(2)}) %all-to-all-start.1) | async-done | bytes 8388640 | tf_op jit(solution)/shard_map/all_to_all | solution.py:36
  334.0 10.4 %fusion.11 = f32[128,3,128]{2,1,0:T(4,128)S(1)} fusion(f32[128,128,128]{2,1,0:T(8,128)} %all-to-all-done.1, s32[128]{0:T(128)S(1)} %eq.49), kind=kOutput, calls=%fused_computation.16 | convolution fusion | flops 75497856 | bytes 8585728 | tf_op jit(solution)/shard_map/ms,srl->rml/dot_general | solution.py:42
  344.5 0.1 copy.21
  344.6 0.2 subtract_convert_fusion
  344.8 4.2 stack.2
  349.0 0.0 copy-start.3
  349.0 49.9 %all-to-all-start.3 = ((bf16[64,128,384]{1,2,0:T(8,128)(2,1)}), bf16[64,128,384]{1,2,0:T(8,128)(2,1)}, u32[]{:S(2)}, u32[]{:S(2)}) async-start(bf16[64,128,384]{1,2,0:T(8,128)(2,1)} %stack.2), calls=%async_computation.3 | async-start | bytes 12582912 | tf_op jit(solution)/shard_map/all_to_all | solution.py:52
  398.8 0.0 copy-done.3
  398.9 188.0 %all-to-all-done.3 = bf16[64,128,384]{1,2,0:T(8,128)(2,1)} async-done(((bf16[64,128,384]{1,2,0:T(8,128)(2,1)}), bf16[64,128,384]{1,2,0:T(8,128)(2,1)}, u32[]{:S(2)}, u32[]{:S(2)}) %all-to-all-start.3) | async-done | bytes 6291488 | tf_op jit(solution)/shard_map/all_to_all | solution.py:52
  586.8 8.6 %copy.23 = bf16[128,192,128]{2,0,1:T(8,128)(2,1)} copy(bf16[128,192,128]{0,2,1:T(8,128)(2,1)} %bitcast.9) | data formatting | bytes 12582912 | tf_op jit(solution)/shard_map/reshape;reshape | solution.py:54
  595.4 3.7 gather_fusion.1
  599.2 0.0 copy-start.2
  599.2 2.4 convolution_bitcast_fusion
  601.6 0.0 copy-done.2
  601.6 3.8 fusion.17
  605.4 0.7 convert_element_type.30
  606.1 31.7 %all-to-all-start.4 = ((bf16[64,2,256]{2,1,0:T(2,128)(2,1)}), bf16[64,2,256]{2,1,0:T(2,128)(2,1)S(1)}, u32[]{:S(2)}, u32[]{:S(2)}) async-start(bf16[64,2,256]{2,1,0:T(2,128)(2,1)} %convert_element_type.30), calls=%async_computation.4 | async-start | bytes 131072 | tf_op jit(solution)/shard_map/all_to_all | solution.py:66
  637.8 0.8 copy.26
  638.6 10.6 %all-to-all-done.4 = bf16[64,2,256]{2,1,0:T(2,128)(2,1)S(1)} async-done(((bf16[64,2,256]{2,1,0:T(2,128)(2,1)}), bf16[64,2,256]{2,1,0:T(2,128)(2,1)S(1)}, u32[]{:S(2)}, u32[]{:S(2)}) %all-to-all-start.4) | async-done | bytes 65568 | tf_op jit(solution)/shard_map/all_to_all | solution.py:66
  649.2 0.6 copy.39
  (7 shorter events, 0.1 us)
Async XLA Ops:
  7.2 40.1 %all-gather.2.cloned.1.call-start = ((), (), s32[]{:S(2)}) async-start(), calls=%async_computation.5 | async-start | bytes 2359296 | tf_op jit(solution)/shard_map/all_gather | solution.py:10
  7.9 28.0 %all-to-all-start = ((bf16[2,64,256]{2,0,1:T(2,128)(2,1)}), bf16[2,64,256]{2,0,1:T(2,128)(2,1)S(1)}, u32[]{:S(2)}, u32[]{:S(2)}) async-start(bf16[2,64,256]{2,0,1:T(2,128)(2,1)} %bitcast.35), calls=%async_computation | async-start | bytes 131072 | tf_op jit(solution)/shard_map/all_to_all | solution.py:9
  35.9 32.7 %all-to-all-start.2 = ((s32[64,2,1]{1,2,0:T(1,128)}), s32[64,2,1]{1,2,0:T(1,128)S(1)}, u32[]{:S(2)}, u32[]{:S(2)}) async-start(s32[64,2,1]{1,2,0:T(1,128)} %bitcast.4), calls=%async_computation.2 | async-start | bytes 65536 | tf_op jit(solution)/shard_map/all_to_all | solution.py:37
  68.6 13.8 %copy-start = (bf16[128,384]{1,0:T(8,128)(2,1)S(1)}, bf16[128,384]{1,0:T(8,128)(2,1)}, u32[]{:S(2)}) copy-start(bf16[128,384]{1,0:T(8,128)(2,1)} %param.10) | copy-start | bytes 294916
  68.6 14.0 %copy-start.1 = (s32[384]{0:T(512)S(1)}, s32[384]{0:T(512)}, u32[]{:S(2)}) copy-start(s32[384]{0:T(512)} %param.11) | copy-start | bytes 4612
  68.6 265.4 %all-to-all-start.1 = ((f32[128,128,128]{2,1,0:T(8,128)}), f32[128,128,128]{2,1,0:T(8,128)}, u32[]{:S(2)}, u32[]{:S(2)}) async-start(f32[128,128,128]{2,1,0:T(8,128)} %scatter_fusion), calls=%async_computation.1 | async-start | bytes 16777216 | tf_op jit(solution)/shard_map/all_to_all | solution.py:36
  349.0 49.9 %copy-start.3 = (s32[64]{0:T(128)S(1)}, s32[64]{0:T(128)}, u32[]{:S(2)}) copy-start(s32[64]{0:T(128)} %param.8) | copy-start | bytes 772
  349.0 237.9 %all-to-all-start.3 = ((bf16[64,128,384]{1,2,0:T(8,128)(2,1)}), bf16[64,128,384]{1,2,0:T(8,128)(2,1)}, u32[]{:S(2)}, u32[]{:S(2)}) async-start(bf16[64,128,384]{1,2,0:T(8,128)(2,1)} %stack.2), calls=%async_computation.3 | async-start | bytes 12582912 | tf_op jit(solution)/shard_map/all_to_all | solution.py:52
  599.2 2.4 copy-start.2
  606.1 43.1 %all-to-all-start.4 = ((bf16[64,2,256]{2,1,0:T(2,128)(2,1)}), bf16[64,2,256]{2,1,0:T(2,128)(2,1)S(1)}, u32[]{:S(2)}, u32[]{:S(2)}) async-start(bf16[64,2,256]{2,1,0:T(2,128)(2,1)} %convert_element_type.30), calls=%async_computation.4 | async-start | bytes 131072 | tf_op jit(solution)/shard_map/all_to_all | solution.py:66
Sparse Core Ops, SparseCore 0:
  10.1 37.0 all-gather.1
